TPU v7x, 32 devices: a whole 2x2x4 slice. The times are simulated.
32 devices in a mesh: grp: 4 (over x, core), seq: 8 (over z, y).
Axes of the slice: x: 2, y: 2, z: 4, core: 2. Of those that a mesh axis runs over, the one named last changes fastest.
Arguments:
- tokens: bfloat16 [32, 64, 128, 512], P(None, 'grp', 'seq'), may hold values from -6 to 6
- cotangent: bfloat16 [32, 64, 128, 512], P(None, 'grp', 'seq'), may hold values from -6 to 6
- gate_weight: bfloat16 [512, 512], replicated, may hold values from -0.25 to 0.25
- first_factor: bfloat16 [4, 32, 32], replicated, may hold values from -1 to 1
- middle_factor: bfloat16 [4, 64, 64], replicated, may hold values from -0.75 to 0.75
- last_factor: bfloat16 [4, 128, 128], replicated, may hold values from -0.5 to 0.5
Outputs:
- d_tokens: bfloat16 [32, 64, 128, 512], P(None, 'grp', 'seq')
- grad_gate: float32 [512, 512], P('seq')
- grad_first: float32 [4, 32, 32], replicated
- grad_middle: float32 [4, 64, 64], P(None, 'grp')
- grad_last: float32 [4, 128, 128], P(None, 'seq')
All inputs are finite; a program needn't handle non-finite values.
Results may differ from a plain program's by a relative error of at most 0.0065.
Values may be sent and summed in bfloat16 or wider, within the bound.
No kernel may reach another device: no remote copies, remote signals or barrier semaphores. Data moves between devices by JAX's collectives and lax.ppermute only.
A program may use at most 192 MiB of HBM per device.

v0:
```python
import math
import jax
import jax.numpy as jnp
from jax import lax
from jax.sharding import PartitionSpec as P

HEADS = 4


def headed(values):
    return values.reshape(values.shape[:-1] + (HEADS, values.shape[-1] // HEADS))


def mixing(weights, values, form):
    result = jnp.einsum(form, weights, headed(values), preferred_element_type=jnp.float32)
    return result.reshape(values.shape)


def contract(left, right, form):
    return jnp.einsum(form, headed(left), headed(right), preferred_element_type=jnp.float32)


def send_last(values):
    return lax.all_to_all(values, "seq", split_axis=0, concat_axis=2, tiled=True)


def send_middle(values):
    return lax.all_to_all(values, "grp", split_axis=2, concat_axis=1, tiled=True)


def return_middle(values):
    return lax.all_to_all(values, "grp", split_axis=1, concat_axis=2, tiled=True)


def return_last(values):
    return lax.all_to_all(values, "seq", split_axis=2, concat_axis=0, tiled=True)


def shards(tokens, cotangent, gate_weight, first_factor, middle_factor, last_factor):
    width = tokens.shape[-1]
    rows = tokens.reshape(-1, width)
    gate = jax.nn.sigmoid(jnp.dot(rows, gate_weight, preferred_element_type=jnp.float32)).reshape(
        tokens.shape
    )
    first_out = mixing(first_factor, tokens, "hab,bjkhe->ajkhe").astype(jnp.bfloat16)
    last_in = send_last(first_out)
    last_out = mixing(last_factor, last_in, "hab,ijbhe->ijahe").astype(jnp.bfloat16)
    middle_in = send_middle(last_out)
    middle_out = mixing(middle_factor, middle_in, "hab,ibkhe->iakhe").astype(jnp.bfloat16)
    mixer = return_last(return_middle(middle_out))
    upstream = cotangent.astype(jnp.float32)
    d_mix = (upstream * gate).astype(jnp.bfloat16)
    d_pre = (upstream * mixer.astype(jnp.float32) * gate * (1.0 - gate)).astype(jnp.bfloat16)
    pre_rows = d_pre.reshape(-1, width)
    gate_part = jnp.einsum("tc,td->cd", rows, pre_rows, preferred_element_type=jnp.float32)
    gate_term = jnp.einsum("td,cd->tc", pre_rows, gate_weight, preferred_element_type=jnp.float32)
    middle_grad_in = send_middle(send_last(d_mix))
    middle_back = mixing(middle_factor, middle_grad_in, "hba,ibkhe->iakhe").astype(jnp.bfloat16)
    middle_part = contract(middle_grad_in, middle_in, "iakhe,ibkhe->hab")
    last_back_in = return_middle(middle_back)
    last_back = mixing(last_factor, last_back_in, "hba,ijbhe->ijahe").astype(jnp.bfloat16)
    last_part = contract(last_back_in, last_in, "ijahe,ijbhe->hab")
    first_back_in = return_last(last_back)
    first_back = mixing(first_factor, first_back_in, "hba,bjkhe->ajkhe")
    first_part = contract(first_back_in, tokens, "ajkhe,bjkhe->hab")
    d_tokens = (
        (first_back.reshape(-1, width) + gate_term).astype(jnp.bfloat16).reshape(tokens.shape)
    )
    total = (
        tokens.shape[0]
        * tokens.shape[1]
        * tokens.shape[2]
        * lax.axis_size("grp")
        * lax.axis_size("seq")
    )
    factor = 1.0 / math.sqrt(total)
    gate_share, last_share = (
        lax.psum_scatter(gate_part, "seq", scatter_dimension=0, tiled=True),
        lax.psum_scatter(last_part, "seq", scatter_dimension=1, tiled=True),
    )
    middle_share = lax.psum_scatter(middle_part, "grp", scatter_dimension=1, tiled=True)
    gate_sum, last_sum, first_half = lax.psum((gate_share, last_share, first_part), "grp")
    middle_sum, first_sum = lax.psum((middle_share, first_half), "seq")
    return (d_tokens, gate_sum * factor, first_sum * factor, middle_sum * factor, last_sum * factor)


def solution(mesh):
    in_specs = (P(None, "grp", "seq", None), P(None, "grp", "seq", None), P(), P(), P(), P())
    out_specs = (
        P(None, "grp", "seq", None),
        P("seq", None),
        P(),
        P(None, "grp", None),
        P(None, "seq", None),
    )
    return jax.shard_map(shards, mesh=mesh, in_specs=in_specs, out_specs=out_specs, check_vma=False)
```

profile of v0, /device:TPU:0, one launch (start us, length us, event | category | flops | bytes accessed | tf_op | source)
XLA Modules:
  0.0 1805.6 jit_solution(3141081176804208275)
XLA Ops:
  7.2 12.5 reshape.70
  19.7 15.6 convert_bitcast_fusion.3
  35.4 28.2 %copy.134 = bf16[32,16,16,4,128]{4,3,2,1,0:T(4,128)(2,1)} copy(bf16[32,16,16,4,128]{4,0,2,1,3:T(8,128)(2,1)S(1)} %convert_bitcast_fusion.3) | data formatting | bytes 16777216 | tf_op jit(solution)/shard_map/convert_element_type | solution.py:45
  63.6 13.1 convert_element_type.79
  76.7 190.4 %all_to_all.120 = bf16[32,16,16,512]{3,2,1,0:T(8,128)(2,1)} all-to-all(bf16[32,16,16,512]{3,2,1,0:T(8,128)(2,1)} %convert_element_type.79), channel_id=1, replica_groups=mesh['grp'=4,'seq'=8] {'seq'}, dimensions={0} | all-to-all | bytes 16777216 | tf_op jit(solution)/shard_map/all_to_all | solution.py:24
  267.1 8.1 copy.229
  275.2 12.6 reshape.71
  287.8 9.5 convert_bitcast_fusion.2
  297.3 10.4 copy.137
  307.7 14.6 copy.138
  322.3 100.5 %all_to_all.121 = bf16[4,16,128,512]{3,1,0,2:T(8,128)(2,1)} all-to-all(bf16[4,16,128,512]{3,1,0,2:T(8,128)(2,1)} %copy.138), channel_id=1, replica_groups=mesh['grp'=4,'seq'=8] {'grp'}, dimensions={2} | all-to-all | bytes 16777216 | tf_op jit(solution)/shard_map/all_to_all | solution.py:28
  422.8 12.3 copy.140
  435.1 12.7 reshape.72
  447.9 14.9 convert_bitcast_fusion.1
  462.8 18.8 %copy.172 = bf16[4,64,32,4,128]{4,3,2,0,1:T(4,128)(2,1)} copy(bf16[4,64,32,4,128]{4,1,2,0,3:T(8,128)(2,1)S(1)} %convert_bitcast_fusion.1) | data formatting | bytes 16777216 | tf_op jit(solution)/shard_map/convert_element_type | solution.py:49
  481.6 13.1 reshape.87
  494.8 100.6 %all_to_all.122 = bf16[4,64,32,512]{3,2,0,1:T(8,128)(2,1)} all-to-all(bf16[4,64,32,512]{3,2,0,1:T(8,128)(2,1)} %reshape.87), channel_id=1, replica_groups=mesh['grp'=4,'seq'=8] {'grp'}, dimensions={1} | all-to-all | bytes 16777216 | tf_op jit(solution)/shard_map/all_to_all | solution.py:32
  595.3 8.3 copy.145
  603.6 11.3 copy.146
  614.9 5.1 all-to-all-start.7
  620.1 11.7 add_divide_fusion
  631.7 171.3 %all-to-all-done.7 = bf16[4,16,128,512]{3,1,0,2:T(8,128)(2,1)} async-done(((bf16[4,16,128,512]{3,1,0,2:T(8,128)(2,1)}), bf16[4,16,128,512]{3,1,0,2:T(8,128)(2,1)}, u32[]{:S(2)}, u32[]{:S(2)}) %all-to-all-start.7) | async-done | bytes 8388640 | tf_op jit(solution)/shard_map/all_to_all | solution.py:36
  803.0 11.4 copy.147
  814.4 11.4 convert_bitcast_fusion
  825.9 7.0 copy.148
  832.9 15.4 fusion.3
  848.3 188.7 %all_to_all.123 = bf16[32,16,16,512]{3,2,1,0:T(8,128)(2,1)} all-to-all(bf16[32,16,16,512]{3,2,1,0:T(8,128)(2,1)} %get-tuple-element.35), channel_id=1, replica_groups=mesh['grp'=4,'seq'=8] {'seq'}, dimensions={0} | all-to-all | bytes 16777216 | tf_op jit(solution)/shard_map/all_to_all | solution.py:24
  1037.0 8.1 copy.117
  1045.1 11.3 copy.118
  1056.5 100.5 %all_to_all.124 = bf16[4,16,128,512]{3,1,0,2:T(8,128)(2,1)} all-to-all(bf16[4,16,128,512]{3,1,0,2:T(8,128)(2,1)} %copy.118), channel_id=1, replica_groups=mesh['grp'=4,'seq'=8] {'grp'}, dimensions={2} | all-to-all | bytes 16777216 | tf_op jit(solution)/shard_map/all_to_all | solution.py:28
  1157.0 12.3 copy.231
  1169.3 12.7 reshape.67
  1182.0 17.9 convert_bitcast_fusion.5
  1199.9 12.1 copy.167
  1212.0 13.1 reshape.86
  1225.1 100.8 %all_to_all.125 = bf16[4,64,32,512]{3,2,0,1:T(8,128)(2,1)} all-to-all(bf16[4,64,32,512]{3,2,0,1:T(8,128)(2,1)} %reshape.86), channel_id=1, replica_groups=mesh['grp'=4,'seq'=8] {'grp'}, dimensions={1} | all-to-all | bytes 16777216 | tf_op jit(solution)/shard_map/all_to_all | solution.py:32
  1325.9 8.3 copy.230
  1334.1 12.6 reshape.68
  1346.7 9.5 convert_bitcast_fusion.4
  1356.2 10.3 copy.126
  1366.6 14.7 copy.127
  1381.2 5.0 all-to-all-start.3
  1386.3 9.5 convolution_bitcast_fusion.1
  1395.8 1.3 copy.174
  1397.2 189.2 %reduce-scatter.10.cloned.1.call-done = f32[64,512]{1,0:T(8,128)} async-done(((f32[512,512]{1,0:T(8,128)}), f32[64,512]{1,0:T(8,128)}) %reduce-scatter.10.cloned.1.call-update) | async-done | bytes 131088
  1586.4 1.8 copy.175
  1588.2 0.0 reduce-scatter.8.cloned.1.call-start
  1588.2 31.5 %all-reduce.4.cloned.1.call-done = f32[64,512]{0,1:T(8,128)} async-done(((f32[64,512]{0,1:T(8,128)}), f32[64,512]{0,1:T(8,128)}) %all-reduce.4.cloned.1.call-update) | async-done | bytes 131088 | tf_op jit(solution)/shard_map/psum | solution.py:82
  1619.7 1.0 broadcast_multiply_fusion
  1620.7 0.8 copy.155
  1621.5 8.8 fusion.35
  1630.3 0.5 reduce-scatter.6.cloned.1.call-start
  1630.8 15.2 fusion.40
  1646.0 15.4 copy.129
  1661.4 12.6 reshape.69
  1674.0 20.3 %convolution_bitcast_fusion = f32[32,16,16,4,128]{4,0,2,1,3:T(8,128)} fusion(bf16[32,16,16,4,128]{4,3,2,1,0:T(4,128)(2,1)} %reshape.69, bf16[4,32,32]{2,1,0:T(8,128)(2,1)S(1)} %copy-done.5), kind=kOutput, calls=%fused_computation.10 | convolution fusion | flops 268435456 | bytes 25174016 | tf_op jit(solution)/shard_map/hba,bjkhe->ajkhe/dot_general | solution.py:15
  1694.3 14.7 fusion.45
  1709.0 11.6 all-reduce.1
  1720.7 38.9 %all-reduce = (f32[4,32,32]{2,1,0:T(8,128)S(1)}, f32[4,16,64]{2,1,0:T(8,128)S(1)}) all-reduce(f32[4,32,32]{2,1,0:T(8,128)S(1)} %get-tuple-element.32, f32[4,16,64]{2,1,0:T(8,128)} %reduce-scatter.6.cloned.1.call-done), channel_id=1, replica_groups=mesh['grp'=4,'seq'=8] {'seq'}, use_global_device_ids=true, to_apply=%region_3.0 | all-reduce | flops 8192 | bytes 65536 | tf_op jit(solution)/shard_map/psum | solution.py:83
  1759.6 0.6 broadcast_multiply_fusion.1
  1760.2 0.6 broadcast_multiply_fusion.3
  1760.8 0.6 broadcast_multiply_fusion.2
  1761.5 21.1 %copy.132 = f32[32,16,16,4,128]{4,3,2,1,0:T(4,128)} copy(f32[32,16,16,4,128]{4,0,2,1,3:T(8,128)} %convolution_bitcast_fusion) | data formatting | bytes 33554432 | tf_op jit(solution)/shard_map/hba,bjkhe->ajkhe/transpose | solution.py:15
  1782.5 16.1 fusion.4
  (21 shorter events, 0.2 us)
Async XLA Ops:
  7.2 612.9 %copy-start = (bf16[512,512]{1,0:T(8,128)(2,1)S(1)}, bf16[512,512]{1,0:T(8,128)(2,1)}, u32[]{:S(2)}) copy-start(bf16[512,512]{1,0:T(8,128)(2,1)} %param.8) | copy-start | bytes 1572868
  7.2 12.6 copy-start.4
  275.2 12.6 copy-start.1
  435.1 12.7 copy-start.3
  614.9 188.1 %all-to-all-start.7 = ((bf16[4,16,128,512]{3,1,0,2:T(8,128)(2,1)}), bf16[4,16,128,512]{3,1,0,2:T(8,128)(2,1)}, u32[]{:S(2)}, u32[]{:S(2)}) async-start(bf16[4,16,128,512]{3,1,0,2:T(8,128)(2,1)} %copy.146), calls=%async_computation.7 | async-start | bytes 16777216 | tf_op jit(solution)/shard_map/all_to_all | solution.py:36
  1334.1 12.6 copy-start.2
  1381.2 264.8 %all-to-all-start.3 = ((bf16[4,16,128,512]{3,1,0,2:T(8,128)(2,1)}), bf16[4,16,128,512]{3,1,0,2:T(8,128)(2,1)}, u32[]{:S(2)}, u32[]{:S(2)}) async-start(bf16[4,16,128,512]{3,1,0,2:T(8,128)(2,1)} %copy.127), calls=%async_computation.3 | async-start | bytes 16777216 | tf_op jit(solution)/shard_map/all_to_all | solution.py:36
  1386.3 200.1 %reduce-scatter.10.cloned.1.call-start = ((), (), s32[]{:S(2)}) async-start(), calls=%async_computation.14 | async-start | bytes 1179648
  1397.2 222.6 %all-reduce.4.cloned.1.call-start = ((), (), s32[]{:S(2)}) async-start(), calls=%async_computation.11 | async-start | bytes 524288 | tf_op jit(solution)/shard_map/psum | solution.py:82
  1588.2 120.9 %reduce-scatter.8.cloned.1.call-start = ((), (), s32[]{:S(2)}) async-start(), calls=%async_computation.13 | async-start | bytes 294912 | tf_op jit(solution)/shard_map/reduce_scatter | solution.py:79
  1630.3 90.4 %reduce-scatter.6.cloned.1.call-start = ((), (), s32[]{:S(2)}) async-start(), calls=%async_computation.12 | async-start | bytes 163840 | tf_op jit(solution)/shard_map/reduce_scatter | solution.py:81
  1661.4 12.6 copy-start.5
Sparse Core Ops, SparseCore 0:
  1397.3 189.0 reduce-scatter.9
  1588.7 30.9 all-reduce.3
  1630.4 62.5 reduce-scatter.7
  1695.2 18.7 reduce-scatter.5
where the time goes:
time: 1820 us; the launch traced here: 1810 us
  blocking collectives  832 us (46%)
  waiting for transfers between devices  392 us (22%)
  local copies, waits for them, and re-layouts  363 us (20%)
  matrix products  164 us (9%)
  other arithmetic  29.7 us (2%)
    all_to_all x2, blocking collectives, send_last(): lax.all_to_all(values, 'seq', split_axis=0, concat_axis=2, tiled=True)  379 us
    all_to_all x2, blocking collectives, return_middle(): lax.all_to_all(values, 'grp', split_axis=1, concat_axis=2, tiled=True)  201 us
    all_to_all x2, blocking collectives, send_middle(): lax.all_to_all(values, 'grp', split_axis=2, concat_axis=1, tiled=True)  201 us
    unnamed x5, waiting for transfers between devices  189 us
    all_to_all x2, waiting for transfers between devices, return_last(): lax.all_to_all(values, 'seq', split_axis=2, concat_axis=0, tiled=True)  171 us
    dot_general x6, matrix products, mixing(): jnp.einsum(form, weights, headed(values), preferred_element_type=jnp.floa...  87.8 us
    reshape x6, local copies, waits for them, and re-layouts, headed(): values.reshape(values.shape[:-1] + (HEADS, values.shape[-1] // HEADS))  75.7 us
    convert_element_type x2, local copies, waits for them, and re-layouts, shards(): mixing(first_factor, tokens, 'hab,bjkhe->ajkhe').astype(jnp.bfloat16)  41.3 us
  transfers between devices with their start and end apart: 6, of which 3 were waited for; matrix products, arithmetic and copies ran while one was open for 6% of the time, Pallas kernels for 0%

commit v1 on v0

--- a/solution.py
+++ b/solution.py
@@ -33,7 +33,13 @@
 
 
 def return_last(values):
-    return lax.all_to_all(values, "seq", split_axis=2, concat_axis=0, tiled=True)
+    name_routes_all = lambda inner_x, in_dim, along_dim: jnp.concatenate(
+        jax.lax.all_to_all(
+            jnp.stack(jnp.split(inner_x, jax.lax.axis_size("seq"), axis=in_dim)), "seq", 0, 0
+        ),
+        axis=along_dim,
+    )
+    return name_routes_all(values, 2, 0)
 
 
 def shards(tokens, cotangent, gate_weight, first_factor, middle_factor, last_factor):

time: 1820 us -> 1880 us (1.033)
  local copies, waits for them, and re-layouts: 363 us -> 429 us
    another operation x0 -> x12, local copies, waits for them, and re-layouts: none -> 124 us  [the longest x11 111 us: return_last(): jnp.stack(jnp.split(inner_x, jax.lax.axis_size('seq'), axis=in_dim))]
    all_to_all x2 -> x0, local copies, waits for them, and re-layouts: 26.8 us -> none  [return_last(): lax.all_to_all(values, 'seq', split_axis=2, concat_axis=0, tiled=True)]
    unnamed x15 -> x35, local copies, waits for them, and re-layouts: 3.86 us -> 29.6 us
    reshape x6 -> x5, local copies, waits for them, and re-layouts: 75.7 us -> 63.2 us  [headed(): values.reshape(values.shape[:-1] + (HEADS, values.shape[-1] // HEADS))]
  transfers between devices with their start and end apart: 6 -> 6, of which waited for: 3 -> 4; matrix products, arithmetic and copies ran while one was open for 6% -> 5% of each run, Pallas kernels for 0% -> 0%
where the time goes in v1:
time: 1880 us; the launch traced here: 1870 us
  blocking collectives  831 us (44%)
  local copies, waits for them, and re-layouts  429 us (23%)
  waiting for transfers between devices  400 us (21%)
  matrix products  164 us (9%)
    all_to_all x2, blocking collectives, send_last(): lax.all_to_all(values, 'seq', split_axis=0, concat_axis=2, tiled=True)  378 us
    all_to_all x2, blocking collectives, return_middle(): lax.all_to_all(values, 'grp', split_axis=1, concat_axis=2, tiled=True)  201 us
    all_to_all x2, blocking collectives, send_middle(): lax.all_to_all(values, 'grp', split_axis=2, concat_axis=1, tiled=True)  201 us
    unnamed x5, waiting for transfers between devices  189 us
    all_to_all x2, waiting for transfers between devices, return_last(): jax.lax.all_to_all(jnp.stack(jnp.split(inner_x, jax.lax.axis_size('seq'),...  171 us
    another operation x11, local copies, waits for them, and re-layouts, return_last(): jnp.stack(jnp.split(inner_x, jax.lax.axis_size('seq'), axis=in_dim))  111 us
    dot_general x6, matrix products, mixing(): jnp.einsum(form, weights, headed(values), preferred_element_type=jnp.floa...  87.9 us
    reshape x5, local copies, waits for them, and re-layouts, headed(): values.reshape(values.shape[:-1] + (HEADS, values.shape[-1] // HEADS))  63.2 us
  transfers between devices with their start and end apart: 6, of which 4 were waited for; matrix products, arithmetic and copies ran while one was open for 5% of the time, Pallas kernels for 0%

profile of v1, /device:TPU:0, one launch (start us, length us, event | category | flops | bytes accessed | tf_op | source)
XLA Modules:
  0.0 1866.8 jit_solution(7707701483854337278)
XLA Ops:
  7.2 12.5 reshape.63
  19.7 15.6 convert_bitcast_fusion.2
  35.4 17.6 copy.99
  53.0 13.1 convert_element_type.73
  66.1 190.5 %all_to_all.106 = bf16[32,16,16,512]{3,2,1,0:T(8,128)(2,1)} all-to-all(bf16[32,16,16,512]{3,2,1,0:T(8,128)(2,1)} %convert_element_type.73), channel_id=1, replica_groups=mesh['grp'=4,'seq'=8] {'seq'}, dimensions={0} | all-to-all | bytes 16777216 | tf_op jit(solution)/shard_map/all_to_all | solution.py:24
  256.6 8.1 copy.190
  264.7 12.6 reshape.64
  277.3 9.5 convert_bitcast_fusion.1
  286.8 10.3 copy.102
  297.2 14.6 copy.103
  311.8 100.5 %all_to_all.107 = bf16[4,16,128,512]{3,1,0,2:T(8,128)(2,1)} all-to-all(bf16[4,16,128,512]{3,1,0,2:T(8,128)(2,1)} %copy.103), channel_id=1, replica_groups=mesh['grp'=4,'seq'=8] {'grp'}, dimensions={2} | all-to-all | bytes 16777216 | tf_op jit(solution)/shard_map/all_to_all | solution.py:28
  412.3 12.3 copy.105
  424.7 12.7 reshape.65
  437.4 14.9 convert_bitcast_fusion
  452.3 18.6 copy.133
  471.0 13.1 reshape.79
  484.1 100.5 %all_to_all.108 = bf16[4,64,32,512]{3,2,0,1:T(8,128)(2,1)} all-to-all(bf16[4,64,32,512]{3,2,0,1:T(8,128)(2,1)} %reshape.79), channel_id=1, replica_groups=mesh['grp'=4,'seq'=8] {'grp'}, dimensions={1} | all-to-all | bytes 16777216 | tf_op jit(solution)/shard_map/all_to_all | solution.py:32
  584.7 8.3 copy.110
  592.9 2.4 fusion.57
  595.4 3.0 fusion.56
  600.6 2.3 fusion.54
  607.2 4.9 all-to-all-start.7
  612.2 11.7 add_divide_fusion
  623.9 171.3 %all-to-all-done.7 = bf16[8,4,16,16,512]{4,3,2,1,0:T(8,128)(2,1)} async-done(((bf16[8,4,16,16,512]{4,3,2,1,0:T(8,128)(2,1)}), bf16[8,4,16,16,512]{4,3,2,1,0:T(8,128)(2,1)}, u32[]{:S(2)}, u32[]{:S(2)}) %all-to-all-start.7) | async-done | bytes 8388640 | tf_op jit(solution)/shard_map/all_to_all | solution.py:37
  795.2 15.0 fusion.3
  810.2 187.1 %all_to_all.109 = bf16[32,16,16,512]{3,2,1,0:T(8,128)(2,1)} all-to-all(bf16[32,16,16,512]{3,2,1,0:T(8,128)(2,1)S(1)} %get-tuple-element.30), channel_id=1, replica_groups=mesh['grp'=4,'seq'=8] {'seq'}, dimensions={0} | all-to-all | bytes 16777216 | tf_op jit(solution)/shard_map/all_to_all | solution.py:24
  997.3 8.1 copy.77
  1005.4 11.4 copy.78
  1016.7 100.5 %all_to_all.110 = bf16[4,16,128,512]{3,1,0,2:T(8,128)(2,1)} all-to-all(bf16[4,16,128,512]{3,1,0,2:T(8,128)(2,1)} %copy.78), channel_id=1, replica_groups=mesh['grp'=4,'seq'=8] {'grp'}, dimensions={2} | all-to-all | bytes 16777216 | tf_op jit(solution)/shard_map/all_to_all | solution.py:28
  1117.3 12.3 copy.192
  1129.6 12.7 reshape.61
  1142.3 17.9 convert_bitcast_fusion.4
  1160.2 12.1 copy.129
  1172.3 13.1 reshape.78
  1185.4 100.9 %all_to_all.111 = bf16[4,64,32,512]{3,2,0,1:T(8,128)(2,1)} all-to-all(bf16[4,64,32,512]{3,2,0,1:T(8,128)(2,1)} %reshape.78), channel_id=1, replica_groups=mesh['grp'=4,'seq'=8] {'grp'}, dimensions={1} | all-to-all | bytes 16777216 | tf_op jit(solution)/shard_map/all_to_all | solution.py:32
  1286.3 8.3 copy.191
  1294.6 12.5 reshape.62
  1307.1 9.5 convert_bitcast_fusion.3
  1316.6 10.3 copy.86
  1327.0 48.7 %slice_bitcast_fusion = (bf16[1,4,16,16,512]{3,4,2,1,0:T(8,128)(2,1)}, bf16[1,4,16,16,512]{3,4,2,1,0:T(8,128)(2,1)}, bf16[1,4,16,16,512]{3,4,2,1,0:T(8,128)(2,1)...) fusion(bf16[4,16,128,512]{2,3,1,0:T(8,128)(2,1)} %bitcast.166), kind=kLoop, calls=%fused_computation.10 | loop fusion | bytes 16777216 | tf_op jit(solution)/shard_map/stack | solution.py:38
  1375.7 6.7 copy.94
  1382.4 6.7 copy.93
  1389.1 7.8 copy.92
  1396.9 7.8 copy.91
  1404.7 7.8 copy.90
  1412.4 7.8 copy.89
  1420.3 7.8 copy.88
  1428.0 7.9 copy.87
  1436.0 2.4 constant_dynamic-update-slice_fusion.7
  1443.0 2.3 constant_dynamic-update-slice_fusion.4
  1449.5 4.9 all-to-all-start.3
  1454.5 9.5 convolution_bitcast_fusion.1
  1465.5 189.2 %reduce-scatter.10.cloned.1.call-done = f32[64,512]{1,0:T(8,128)} async-done(((f32[512,512]{1,0:T(8,128)}), f32[64,512]{1,0:T(8,128)}) %reduce-scatter.10.cloned.1.call-update) | async-done | bytes 131088
  1656.4 31.5 %all-reduce.4.cloned.1.call-done = f32[64,512]{0,1:T(8,128)} async-done(((f32[64,512]{0,1:T(8,128)}), f32[64,512]{0,1:T(8,128)}) %all-reduce.4.cloned.1.call-update) | async-done | bytes 131088 | tf_op jit(solution)/shard_map/psum | solution.py:88
  1689.7 8.8 fusion.35
  1698.6 15.2 fusion.40
  1713.8 12.8 reshape_reshape.7
  1726.6 20.4 %convolution_bitcast_fusion = f32[32,16,16,4,128]{4,0,2,1,3:T(8,128)} fusion(bf16[32,16,16,4,128]{4,3,2,1,0:T(4,128)(2,1)} %reshape_reshape.7, bf16[4,32,32]{2,1,0:T(8,128)(2,1)S(1)} %copy-done.8), kind=kOutput, calls=%fused_computation.9 | convolution fusion | flops 268435456 | bytes 25174016 | tf_op jit(solution)/shard_map/hba,bjkhe->ajkhe/dot_general | solution.py:15
  1747.0 14.9 fusion.45
  1762.0 12.1 all-reduce.1
  1774.1 8.2 reduce-scatter.6.cloned.1.call-done
  1782.2 38.8 %all-reduce = (f32[4,32,32]{2,1,0:T(8,128)S(1)}, f32[4,16,64]{2,1,0:T(8,128)S(1)}) all-reduce(f32[4,32,32]{2,1,0:T(8,128)S(1)} %get-tuple-element.27, f32[4,16,64]{2,1,0:T(8,128)} %reduce-scatter.6.cloned.1.call-done), channel_id=1, replica_groups=mesh['grp'=4,'seq'=8] {'seq'}, use_global_device_ids=true, to_apply=%region_3.0 | all-reduce | flops 8192 | bytes 65536 | tf_op jit(solution)/shard_map/psum | solution.py:89
  1822.9 21.1 %copy.97 = f32[32,16,16,4,128]{4,3,2,1,0:T(4,128)} copy(f32[32,16,16,4,128]{4,0,2,1,3:T(8,128)} %convolution_bitcast_fusion) | data formatting | bytes 33554432 | tf_op jit(solution)/shard_map/hba,bjkhe->ajkhe/transpose | solution.py:15
  1844.0 16.1 fusion.4
  (46 shorter events, 22.3 us)
Async XLA Ops:
  7.2 605.0 %copy-start = (bf16[512,512]{1,0:T(8,128)(2,1)S(1)}, bf16[512,512]{1,0:T(8,128)(2,1)}, u32[]{:S(2)}) copy-start(bf16[512,512]{1,0:T(8,128)(2,1)} %param.8) | copy-start | bytes 1572868
  7.2 12.6 copy-start.7
  264.7 12.6 copy-start.4
  424.7 12.7 copy-start.6
  592.9 10.0 copy-start.1
  607.2 187.9 %all-to-all-start.7 = ((bf16[8,4,16,16,512]{4,3,2,1,0:T(8,128)(2,1)}), bf16[8,4,16,16,512]{4,3,2,1,0:T(8,128)(2,1)}, u32[]{:S(2)}, u32[]{:S(2)}) async-start(bf16[8,4,16,16,512]{4,3,2,1,0:T(8,128)(2,1)} %fusion.50), calls=%async_computation.7 | async-start | bytes 16777216 | tf_op jit(solution)/shard_map/all_to_all | solution.py:37
  1294.6 12.5 copy-start.5
  1436.0 9.3 copy-start.3
  1436.0 10.4 copy-start.2
  1449.5 264.2 %all-to-all-start.3 = ((bf16[8,4,16,16,512]{4,3,2,1,0:T(8,128)(2,1)}), bf16[8,4,16,16,512]{4,3,2,1,0:T(8,128)(2,1)}, u32[]{:S(2)}, u32[]{:S(2)}) async-start(bf16[8,4,16,16,512]{4,3,2,1,0:T(8,128)(2,1)} %constant_dynamic-update-slice_fusion), calls=%async_computation.3 | async-start | bytes 16777216 | tf_op jit(solution)/shard_map/all_to_all | solution.py:37
  1454.5 200.1 %reduce-scatter.10.cloned.1.call-start = ((), (), s32[]{:S(2)}) async-start(), calls=%async_computation.14 | async-start | bytes 1179648
  1465.4 222.6 %all-reduce.4.cloned.1.call-start = ((), (), s32[]{:S(2)}) async-start(), calls=%async_computation.11 | async-start | bytes 524288 | tf_op jit(solution)/shard_map/psum | solution.py:88
  1656.4 105.6 %reduce-scatter.8.cloned.1.call-start = ((), (), s32[]{:S(2)}) async-start(), calls=%async_computation.13 | async-start | bytes 294912 | tf_op jit(solution)/shard_map/reduce_scatter | solution.py:85
  1698.5 83.7 %reduce-scatter.6.cloned.1.call-start = ((), (), s32[]{:S(2)}) async-start(), calls=%async_computation.12 | async-start | bytes 163840 | tf_op jit(solution)/shard_map/reduce_scatter | solution.py:87
  1713.8 12.8 copy-start.8
Sparse Core Ops, SparseCore 0:
  1465.5 189.0 reduce-scatter.9
  1656.9 30.9 all-reduce.3
  1698.7 62.5 reduce-scatter.7
  1763.5 18.6 reduce-scatter.5
